TPU v7x, 512 devices: a whole 4x8x8 slice. The times are simulated.
512 devices in a mesh: tx: 16 (over z, core), ty: 8 (over y_hi, x), mode: 4 (over y_lo).
Axes of the slice: x: 4, y: 8 (y_hi: 2, y_lo: 4; y = y_hi * 4 + y_lo), z: 8, core: 2. Of those that a mesh axis runs over, the one named last changes fastest.
Arguments:
- object_field: float32 [2, 2048, 2048], P(None, 'tx', 'ty'), may hold values from -5 to 5
- probe: float32 [2, 8, 256, 256], P(None, 'mode'), may hold values from -1.5 to 1.5
- amplitudes: bfloat16 [16, 8, 2, 256, 256], P('tx', 'ty'), may hold values from 0.29882812 to 2.5
- centers: int32 [16, 8, 2, 2], P('tx', 'ty'), may hold values from 0 to 255, as said below
- live: int32 [16, 8], P('tx', 'ty'), may hold values from 1 to 2, as said below
Outputs:
- updated: float32 [2, 2048, 2048], P(None, 'tx', 'ty')
Inputs may be any that keep to these rules, and one draw needn't show every extreme that they name: `centers`: the first component is under 128, the second under 256; some live slot sits at offsets (127, 255) and some at (0, 0). A tile's positions fill its slots 0 to live - 1; some tile has all 2 slots live and some only one.
All inputs are finite; a program needn't handle non-finite values.
Results may differ from a plain program's by a relative error of at most 0.006.
Values may be sent and summed in bfloat16 or wider, within the bound.
A program may use at most 64 MiB of HBM per device.

v0:
```python
import math
import jax
import jax.numpy as jnp
from jax import lax
from jax.sharding import PartitionSpec as P

power_floor = 0.01
regularizer = 0.1


def padded_2(block, sides, width):
    for axis, dim in sides:
        count = lax.axis_size(axis)
        forward = [(i, i + 1) for i in range(count - 1)]
        backward = [(target, source) for source, target in forward]
        low = lax.ppermute(
            lax.slice_in_dim(block, block.shape[dim] - width, None, axis=dim), axis, forward
        )
        high = lax.ppermute(lax.slice_in_dim(block, 0, width, axis=dim), axis, backward)
        block = jnp.concatenate([low, block, high], axis=dim)
    return block


def dft_tables(pattern_side):
    index_line = jnp.arange(pattern_side, dtype=jnp.int32)
    product_table = index_line[:, None] * index_line[None, :] % pattern_side
    angle_table = product_table.astype(jnp.float32) * (2.0 * math.pi / pattern_side)
    scaling = 1.0 / math.sqrt(pattern_side)
    table_real = (jnp.cos(angle_table) * scaling).astype(jnp.bfloat16)
    table_imaginary = (-jnp.sin(angle_table) * scaling).astype(jnp.bfloat16)
    return (table_real, table_imaginary)


def left_mult(matrix, signal):
    return jnp.einsum("uv,kvw->kuw", matrix, signal, preferred_element_type=jnp.float32)


def right_mult(signal, matrix):
    return jnp.einsum("kuv,vw->kuw", signal, matrix, preferred_element_type=jnp.float32)


def left_apply(matrix_real, matrix_imaginary, signal_real, signal_imaginary):
    return (
        left_mult(matrix_real, signal_real) - left_mult(matrix_imaginary, signal_imaginary),
        left_mult(matrix_real, signal_imaginary) + left_mult(matrix_imaginary, signal_real),
    )


def right_apply(matrix_real, matrix_imaginary, signal_real, signal_imaginary):
    return (
        right_mult(signal_real, matrix_real) - right_mult(signal_imaginary, matrix_imaginary),
        right_mult(signal_real, matrix_imaginary) + right_mult(signal_imaginary, matrix_real),
    )


def forward_wave(patch, probe_real, probe_imaginary, table_real, table_imaginary):
    patch_real = patch[0].astype(jnp.float32)
    patch_imaginary = patch[1].astype(jnp.float32)
    exit_real = (probe_real * patch_real - probe_imaginary * patch_imaginary).astype(jnp.bfloat16)
    exit_imaginary = (probe_real * patch_imaginary + probe_imaginary * patch_real).astype(
        jnp.bfloat16
    )
    half_real, half_imaginary = left_apply(table_real, table_imaginary, exit_real, exit_imaginary)
    far_real, far_imaginary = right_apply(
        table_real,
        table_imaginary,
        half_real.astype(jnp.bfloat16),
        half_imaginary.astype(jnp.bfloat16),
    )
    return (exit_real, exit_imaginary, far_real, far_imaginary)


def backward_wave(
    far_real,
    far_imaginary,
    power,
    amplitude,
    exit_real,
    exit_imaginary,
    probe_real,
    probe_imaginary,
    table_real,
    table_imaginary,
):
    factor = amplitude.astype(jnp.float32) / jnp.sqrt(power + power_floor)
    fixed_real = (far_real * factor).astype(jnp.bfloat16)
    fixed_imaginary = (far_imaginary * factor).astype(jnp.bfloat16)
    back_half_real, back_half_imaginary = left_apply(
        table_real, -table_imaginary, fixed_real, fixed_imaginary
    )
    back_real, back_imaginary = right_apply(
        table_real,
        -table_imaginary,
        back_half_real.astype(jnp.bfloat16),
        back_half_imaginary.astype(jnp.bfloat16),
    )
    diff_real = back_real - exit_real.astype(jnp.float32)
    diff_imaginary = back_imaginary - exit_imaginary.astype(jnp.float32)
    grad_real = jnp.sum(probe_real * diff_real + probe_imaginary * diff_imaginary, axis=0)
    grad_imaginary = jnp.sum(probe_real * diff_imaginary - probe_imaginary * diff_real, axis=0)
    return (grad_real, grad_imaginary)


def on_device(object_field, probe, amplitudes, centers, live):
    pattern_side = probe.shape[2]
    half_width = pattern_side // 2
    tile_rows = object_field.shape[1]
    tile_cols = object_field.shape[2]
    slot_total = centers.shape[2]
    channels = 3
    table_real, table_imaginary = dft_tables(pattern_side)
    object_low = object_field.astype(jnp.bfloat16)
    padded = padded_2(object_low, (("tx", 1), ("ty", 2)), half_width)
    live_count = live[0, 0]
    anchor = jnp.zeros((), jnp.int32)
    extended = jnp.zeros(
        (channels, tile_rows + pattern_side, tile_cols + pattern_side), jnp.float32
    )

    def place_of(slot_index):
        return (centers[0, 0, slot_index, 0], centers[0, 0, slot_index, 1])

    def patch_of(row_at, col_at):
        return lax.dynamic_slice(padded, (anchor, row_at, col_at), (2, pattern_side, pattern_side))

    def deposit(extended, row_at, col_at, grad_real, grad_imaginary, weight):
        block = jnp.stack([grad_real, grad_imaginary, weight])
        current = lax.dynamic_slice(
            extended, (anchor, row_at, col_at), (channels, pattern_side, pattern_side)
        )
        return lax.dynamic_update_slice(extended, current + block, (anchor, row_at, col_at))

    probe_real = probe[0]
    probe_imaginary = probe[1]
    modes_here = probe.shape[1]
    weight = jnp.sum(probe_real * probe_real + probe_imaginary * probe_imaginary, axis=0)
    far_store = jnp.zeros((slot_total, 2, modes_here, pattern_side, pattern_side), jnp.float32)
    exit_store = jnp.zeros((slot_total, 2, modes_here, pattern_side, pattern_side), jnp.bfloat16)
    power_part = jnp.zeros((slot_total, pattern_side, pattern_side), jnp.float32)

    def look(slot_index, state):
        far_store, exit_store, power_part = state
        row_at, col_at = place_of(slot_index)
        exit_real, exit_imaginary, far_real, far_imaginary = forward_wave(
            patch_of(row_at, col_at), probe_real, probe_imaginary, table_real, table_imaginary
        )
        far_store = lax.dynamic_update_index_in_dim(
            far_store, jnp.stack([far_real, far_imaginary]), slot_index, 0
        )
        exit_store = lax.dynamic_update_index_in_dim(
            exit_store, jnp.stack([exit_real, exit_imaginary]), slot_index, 0
        )
        power_slot = jnp.sum(far_real * far_real + far_imaginary * far_imaginary, axis=0)
        power_part = lax.dynamic_update_index_in_dim(power_part, power_slot, slot_index, 0)
        return (far_store, exit_store, power_part)

    far_store, exit_store, power_part = lax.fori_loop(
        0, live_count, look, (far_store, exit_store, power_part)
    )
    power_all = lax.psum(power_part.astype(jnp.bfloat16), "mode").astype(jnp.float32)

    def apply_slot(slot_index, extended):
        row_at, col_at = place_of(slot_index)
        far_slot = lax.dynamic_index_in_dim(far_store, slot_index, 0, keepdims=False)
        exit_slot = lax.dynamic_index_in_dim(exit_store, slot_index, 0, keepdims=False)
        power = lax.dynamic_index_in_dim(power_all, slot_index, 0, keepdims=False)
        amplitude = lax.dynamic_index_in_dim(amplitudes[0, 0], slot_index, 0, keepdims=False)
        grad_real, grad_imaginary = backward_wave(
            far_slot[0],
            far_slot[1],
            power,
            amplitude,
            exit_slot[0],
            exit_slot[1],
            probe_real,
            probe_imaginary,
            table_real,
            table_imaginary,
        )
        return deposit(extended, row_at, col_at, grad_real, grad_imaginary, weight)

    extended = lax.fori_loop(0, live_count, apply_slot, extended)
    rows_out = jnp.concatenate(
        [extended[:, :half_width, :], extended[:, tile_rows + half_width :, :]], axis=1
    )
    rows_back = padded_2(rows_out.astype(jnp.bfloat16), (("tx", 1),), half_width).astype(
        rows_out.dtype
    )
    inner = extended[:, half_width : half_width + tile_rows, :]
    inner = inner.at[:, :half_width, :].add(rows_back[:, :half_width, :])
    inner = inner.at[:, tile_rows - half_width :, :].add(rows_back[:, 3 * half_width :, :])
    cols_out = jnp.concatenate(
        [inner[:, :, :half_width], inner[:, :, tile_cols + half_width :]], axis=2
    )
    cols_back = padded_2(cols_out.astype(jnp.bfloat16), (("ty", 2),), half_width).astype(
        cols_out.dtype
    )
    core = inner[:, :, half_width : half_width + tile_cols]
    core = core.at[:, :, :half_width].add(cols_back[:, :, :half_width])
    core = core.at[:, :, tile_cols - half_width :].add(cols_back[:, :, 3 * half_width :])
    summed = lax.psum(core.astype(jnp.bfloat16), "mode").astype(jnp.float32)
    return object_field + summed[:2] / (summed[2] + regularizer)


def solution(mesh):
    return jax.shard_map(
        on_device,
        mesh=mesh,
        in_specs=(
            P(None, "tx", "ty"),
            P(None, "mode", None, None),
            P("tx", "ty", None, None, None),
            P("tx", "ty", None, None),
            P("tx", "ty"),
        ),
        out_specs=P(None, "tx", "ty"),
        check_vma=False,
    )
```

profile of v0, /device:TPU:2, one launch (start us, length us, event | category | flops | bytes accessed | tf_op | source)
XLA Modules:
  0.0 308.4 jit_solution(16685017725092557172)
XLA Ops:
  9.0 3.0 collective-permute-start
  13.1 3.4 %collective-permute-start.2 = (bf16[2,384,128]{1,2,0:T(8,128)(2,1)S(1)}, bf16[2,384,128]{1,2,0:T(8,128)(2,1)S(1)}, u32[]{:S(2)}, u32[]{:S(2)}) collective-permute-start(bf16[2,384,128]{1,2,0:T(8,128)(2,1)S(1)} %get-tuple-element.527), channel_id=1, source_target_pairs={{0,4},{4,8},{8,12},{12,16},{16,20},{20,24},{24,28},{1,5},{5,9},{9,... | collective-permute-start | bytes 589832 | tf_op jit(solution)/shard_map/ppermute | solution.py:16
  16.5 5.7 %collective-permute-start.3 = (bf16[2,384,128]{1,2,0:T(8,128)(2,1)S(1)}, bf16[2,384,128]{1,2,0:T(8,128)(2,1)}, u32[]{:S(2)}, u32[]{:S(2)}) collective-permute-start(bf16[2,384,128]{1,2,0:T(8,128)(2,1)S(1)} %get-tuple-element.528), channel_id=1, source_target_pairs={{4,0},{8,4},{12,8},{16,12},{20,16},{24,20},{28,24},{5,1},{9,5},{13... | collective-permute-start | bytes 589832 | tf_op jit(solution)/shard_map/ppermute | solution.py:19
  23.3 2.4 collective-permute-done.2
  31.9 39.6 %while.36 = (s32[]{:T(128)}, f32[2,2,2,256,256]{4,3,2,1,0:T(8,128)}, bf16[2,2,2,256,256]{3,4,2,1,0:T(8,128)(2,1)}, bf16[2,256,256]{1,2,0:T(8,128)(2,1)}, s32[]{:...) while((s32[]{:T(128)}, ...), condition=%wide.region_2.3_spmd.clone.clone, body=%wide.region_0.2_spmd.clone.clone.sunk | while | flops 550305792 | bytes 17170740 | solution.py:157
  46.0 1.9 add_reduce_fusion.5
  65.5 1.9 add_reduce_fusion.5
  71.6 2.0 add_reduce_fusion.2
  73.6 66.5 %all-reduce.3.cloned.1.call-done = bf16[2,256,256]{1,2,0:T(8,128)(2,1)} async-done(((bf16[2,256,256]{1,2,0:T(8,128)(2,1)}), bf16[2,256,256]{1,2,0:T(8,128)(2,1)}) %all-reduce.3.cloned.1.call-update) | async-done | bytes 262160 | tf_op jit(solution)/shard_map/psum | solution.py:160
  140.2 1.8 convert_element_type.192
  142.3 78.2 %while.37 = (s32[]{:T(128)}, f32[3,384,512]{2,1,0:T(8,128)S(1)}, s32[]{:T(128)}, s32[1,1,2,2]{3,2,1,0:T(2,128)S(1)}, f32[2,2,2,256,256]{4,3,2,1,0:T(8,128)}, /*i...) while((s32[]{:T(128)}, f32[3,384,512]{2,1,0:T(8,128)S(1)}, ...), condition=%wide.region_8.9_spmd.clone.clone, body=%wide.region_5.8_spmd.clone.clone.sunk | while | flops 550371328 | bytes 32899572 | solution.py:182
  148.6 1.7 fusion.264
  155.5 2.2 fusion.268
  157.7 2.3 fusion.269
  168.7 13.0 %dynamic_update_slice.35 = f32[3,384,512]{2,1,0:T(8,128)S(1)} dynamic-update-slice(f32[3,384,512]{2,1,0:T(8,128)S(1)} %get-tuple-element.752, f32[3,256,256]{2,1,0:T(8,128)S(1)} %maximum_add_fusion.2, s32[]{:T(128)} %constant.211.clone.1..sunk.1, s32[]{:T(128)S(6)} %select_n.188, s32[]{:T(128)S(6)} %select_n.189) | dynamic-update-slice | bytes 1572868 | tf_op jit(solution)/shard_map/while/body/dynamic_update_slice | solution.py:131
  187.8 1.7 fusion.264
  194.8 2.2 fusion.268
  197.0 2.3 fusion.269
  207.9 12.0 %dynamic_update_slice.35 = f32[3,384,512]{2,1,0:T(8,128)S(1)} dynamic-update-slice(f32[3,384,512]{2,1,0:T(8,128)S(1)} %get-tuple-element.752, f32[3,256,256]{2,1,0:T(8,128)S(1)} %maximum_add_fusion.2, s32[]{:T(128)} %constant.211.clone.1..sunk.1, s32[]{:T(128)S(6)} %select_n.188, s32[]{:T(128)S(6)} %select_n.189) | dynamic-update-slice | bytes 1572868 | tf_op jit(solution)/shard_map/while/body/dynamic_update_slice | solution.py:131
  223.3 2.3 collective-permute-done.5
  225.9 2.1 collective-permute-start.6
  227.9 3.9 %collective-permute-start.7 = (bf16[3,128,128]{2,1,0:T(8,128)(2,1)S(1)}, bf16[3,128,128]{2,1,0:T(8,128)(2,1)S(1)}, u32[]{:S(2)}, u32[]{:S(2)}) collective-permute-start(bf16[3,128,128]{2,1,0:T(8,128)(2,1)S(1)} %get-tuple-element.526), channel_id=1, source_target_pairs={{4,0},{8,4},{12,8},{16,12},{20,16},{24,20},{28,24},{5,1},{9,5},{13... | collective-permute-start | bytes 294920 | tf_op jit(solution)/shard_map/ppermute | solution.py:19
  232.5 1.9 collective-permute-done.7
  235.3 64.6 %all-reduce.5.cloned.1.call-done = bf16[3,128,256]{2,1,0:T(8,128)(2,1)} async-done(((bf16[3,128,256]{2,1,0:T(8,128)(2,1)}), bf16[3,128,256]{2,1,0:T(8,128)(2,1)}) %all-reduce.5.cloned.1.call-update) | async-done | bytes 196624 | tf_op jit(solution)/shard_map/psum | solution.py:201
  (140 shorter events, 73.7 us)
Async XLA Ops:
  6.5 15.7 %copy-start.8 = (f32[2,2,256,256]{3,2,1,0:T(8,128)S(1)}, f32[2,2,256,256]{3,2,1,0:T(8,128)}, u32[]{:S(2)}) copy-start(f32[2,2,256,256]{3,2,1,0:T(8,128)} %param.22) | copy-start | bytes 3145732
  6.5 133.6 %all-reduce.3.cloned.1.call-start = ((), (), s32[]{:S(2)}) async-start(), calls=%async_computation | async-start | bytes 524288 | tf_op jit(solution)/shard_map/psum | solution.py:160
  7.7 4.3 %collective-permute-start.1 = (bf16[2,128,256]{1,2,0:T(8,128)(2,1)S(1)}, bf16[2,128,256]{1,2,0:T(8,128)(2,1)S(1)}, u32[]{:S(2)}, u32[]{:S(2)}) collective-permute-start(bf16[2,128,256]{1,2,0:T(8,128)(2,1)S(1)} %copy.14), channel_id=1, source_target_pairs={{32,0},{64,32},{96,64},{128,96},{160,128},{192,160},{224,192},{256... | collective-permute-start | bytes 393224 | tf_op jit(solution)/shard_map/ppermute | solution.py:19
  9.0 4.0 %collective-permute-start = (bf16[2,128,256]{1,2,0:T(8,128)(2,1)S(1)}, bf16[2,128,256]{1,2,0:T(8,128)(2,1)S(1)}, u32[]{:S(2)}, u32[]{:S(2)}) collective-permute-start(bf16[2,128,256]{1,2,0:T(8,128)(2,1)S(1)} %copy.14), channel_id=1, source_target_pairs={{0,32},{32,64},{64,96},{96,128},{128,160},{160,192},{192,224},{224... | collective-permute-start | bytes 393224 | tf_op jit(solution)/shard_map/ppermute | solution.py:16
  12.1 10.3 %copy-start.10 = (bf16[2,128,256]{1,2,0:T(8,128)(2,1)}, bf16[2,128,256]{1,2,0:T(8,128)(2,1)S(1)}, u32[]{:S(2)}) copy-start(bf16[2,128,256]{1,2,0:T(8,128)(2,1)S(1)} %collective-permute-done.1) | copy-start | bytes 393220
  13.0 9.3 %copy-start.12 = (bf16[2,128,256]{1,2,0:T(8,128)(2,1)}, bf16[2,128,256]{1,2,0:T(8,128)(2,1)S(1)}, u32[]{:S(2)}) copy-start(bf16[2,128,256]{1,2,0:T(8,128)(2,1)S(1)} %collective-permute-done) | copy-start | bytes 393220
  13.1 12.6 %collective-permute-start.2 = (bf16[2,384,128]{1,2,0:T(8,128)(2,1)S(1)}, bf16[2,384,128]{1,2,0:T(8,128)(2,1)S(1)}, u32[]{:S(2)}, u32[]{:S(2)}) collective-permute-start(bf16[2,384,128]{1,2,0:T(8,128)(2,1)S(1)} %get-tuple-element.527), channel_id=1, source_target_pairs={{0,4},{4,8},{8,12},{12,16},{16,20},{20,24},{24,28},{1,5},{5,9},{9,... | collective-permute-start | bytes 589832 | tf_op jit(solution)/shard_map/ppermute | solution.py:16
  16.5 11.0 %collective-permute-start.3 = (bf16[2,384,128]{1,2,0:T(8,128)(2,1)S(1)}, bf16[2,384,128]{1,2,0:T(8,128)(2,1)}, u32[]{:S(2)}, u32[]{:S(2)}) collective-permute-start(bf16[2,384,128]{1,2,0:T(8,128)(2,1)S(1)} %get-tuple-element.528), channel_id=1, source_target_pairs={{4,0},{8,4},{12,8},{16,12},{20,16},{24,20},{28,24},{5,1},{9,5},{13... | collective-permute-start | bytes 589832 | tf_op jit(solution)/shard_map/ppermute | solution.py:19
  22.4 8.1 %copy-start.3 = (f32[2,256,256]{2,1,0:T(8,128)}, f32[2,256,256]{2,1,0:T(8,128)S(1)}, u32[]{:S(2)}) copy-start(f32[2,256,256]{2,1,0:T(8,128)S(1)} %get-tuple-element.742) | copy-start | bytes 1572868
  22.4 5.1 %copy-start.11 = (bf16[2,128,256]{1,2,0:T(8,128)(2,1)S(1)}, bf16[2,128,256]{1,2,0:T(8,128)(2,1)}, u32[]{:S(2)}) copy-start(bf16[2,128,256]{1,2,0:T(8,128)(2,1)} %copy-done.10) | copy-start | bytes 393220
  22.4 5.1 %copy-start.13 = (bf16[2,128,256]{1,2,0:T(8,128)(2,1)S(1)}, bf16[2,128,256]{1,2,0:T(8,128)(2,1)}, u32[]{:S(2)}) copy-start(bf16[2,128,256]{1,2,0:T(8,128)(2,1)} %copy-done.12) | copy-start | bytes 393220
  28.6 3.3 %copy-start.15 = (s32[1,1,2,2]{3,2,1,0:T(2,128)S(1)}, s32[1,1,2,2]{3,2,1,0:T(2,128)}, u32[]{:S(2)}) copy-start(s32[1,1,2,2]{3,2,1,0:T(2,128)} %param.24) | copy-start | bytes 52
  71.6 228.3 %all-reduce.5.cloned.1.call-start = ((), (), s32[]{:S(2)}) async-start(), calls=%async_computation.1 | async-start | bytes 393216 | tf_op jit(solution)/shard_map/psum | solution.py:201
  155.5 4.5 %copy-start.5 = (f32[1,1,2,256,256]{3,4,2,1,0:T(8,128)S(1)}, f32[1,1,2,256,256]{3,4,2,1,0:T(8,128)}, u32[]{:S(2)}) copy-start(f32[1,1,2,256,256]{3,4,2,1,0:T(8,128)} %copy.46) | copy-start | bytes 1572868 | tf_op jit(solution)/shard_map/while
  155.5 4.5 %copy-start.7 = (f32[256,256]{0,1:T(8,128)S(1)}, f32[256,256]{0,1:T(8,128)}, u32[]{:S(2)}) copy-start(f32[256,256]{0,1:T(8,128)} %fusion.264) | copy-start | bytes 786436 | tf_op jit(solution)/shard_map/while
  161.2 3.6 %copy-start.6 = (bf16[1,1,2,256,256]{4,3,2,1,0:T(8,128)(2,1)S(1)}, bf16[1,1,2,256,256]{4,3,2,1,0:T(8,128)(2,1)}, u32[]{:S(2)}) copy-start(bf16[1,1,2,256,256]{4,3,2,1,0:T(8,128)(2,1)} %copy.49) | copy-start | bytes 786436 | tf_op jit(solution)/shard_map/while
  194.7 4.5 %copy-start.5 = (f32[1,1,2,256,256]{3,4,2,1,0:T(8,128)S(1)}, f32[1,1,2,256,256]{3,4,2,1,0:T(8,128)}, u32[]{:S(2)}) copy-start(f32[1,1,2,256,256]{3,4,2,1,0:T(8,128)} %copy.46) | copy-start | bytes 1572868 | tf_op jit(solution)/shard_map/while
  194.8 4.5 %copy-start.7 = (f32[256,256]{0,1:T(8,128)S(1)}, f32[256,256]{0,1:T(8,128)}, u32[]{:S(2)}) copy-start(f32[256,256]{0,1:T(8,128)} %fusion.264) | copy-start | bytes 786436 | tf_op jit(solution)/shard_map/while
  200.5 3.6 %copy-start.6 = (bf16[1,1,2,256,256]{4,3,2,1,0:T(8,128)(2,1)S(1)}, bf16[1,1,2,256,256]{4,3,2,1,0:T(8,128)(2,1)}, u32[]{:S(2)}) copy-start(bf16[1,1,2,256,256]{4,3,2,1,0:T(8,128)(2,1)} %copy.49) | copy-start | bytes 786436 | tf_op jit(solution)/shard_map/while
  220.7 2.6 collective-permute-start.4
  222.0 3.6 %collective-permute-start.5 = (bf16[3,128,512]{2,1,0:T(8,128)(2,1)S(1)}, bf16[3,128,512]{2,1,0:T(8,128)(2,1)S(1)}, u32[]{:S(2)}, u32[]{:S(2)}) collective-permute-start(bf16[3,128,512]{2,1,0:T(8,128)(2,1)S(1)} %get-tuple-element.522), channel_id=1, source_target_pairs={{32,0},{64,32},{96,64},{128,96},{160,128},{192,160},{224,192},{256... | collective-permute-start | bytes 1179656 | tf_op jit(solution)/shard_map/ppermute | solution.py:19
  225.9 75.0 %copy-start.9 = (f32[2,128,256]{2,1,0:T(8,128)S(1)}, f32[2,128,256]{2,1,0:T(8,128)}, u32[]{:S(2)}) copy-start(f32[2,128,256]{2,1,0:T(8,128)} %param.21) | copy-start | bytes 786436
  225.9 6.6 %collective-permute-start.6 = (bf16[3,128,128]{2,1,0:T(8,128)(2,1)S(1)}, bf16[3,128,128]{2,1,0:T(8,128)(2,1)S(1)}, u32[]{:S(2)}, u32[]{:S(2)}) collective-permute-start(bf16[3,128,128]{2,1,0:T(8,128)(2,1)S(1)} %get-tuple-element.525), channel_id=1, source_target_pairs={{0,4},{4,8},{8,12},{12,16},{16,20},{20,24},{24,28},{1,5},{5,9},{9,... | collective-permute-start | bytes 294920 | tf_op jit(solution)/shard_map/ppermute | solution.py:16
  227.9 6.5 %collective-permute-start.7 = (bf16[3,128,128]{2,1,0:T(8,128)(2,1)S(1)}, bf16[3,128,128]{2,1,0:T(8,128)(2,1)S(1)}, u32[]{:S(2)}, u32[]{:S(2)}) collective-permute-start(bf16[3,128,128]{2,1,0:T(8,128)(2,1)S(1)} %get-tuple-element.526), channel_id=1, source_target_pairs={{4,0},{8,4},{12,8},{16,12},{20,16},{24,20},{28,24},{5,1},{9,5},{13... | collective-permute-start | bytes 294920 | tf_op jit(solution)/shard_map/ppermute | solution.py:19
  (8 other events, 16.0 us)
Sparse Core Ops, SparseCore 0:
  71.7 68.4 all-reduce.2
  235.4 64.4 all-reduce.4
where the time goes:
time: 310 us; the launch traced here: 308 us
  waiting for transfers between devices  140 us (45%)
  local copies, waits for them, and re-layouts  49.8 us (16%)
  matrix products  43.8 us (14%)
  starting transfers between devices  22 us (7%)
  loops' own time  20.2 us (7%)
  other arithmetic  18.4 us (6%)
  between operations  13.7 us (4%)
    psum x1, waiting for transfers between devices, on_device(): lax.psum(power_part.astype(jnp.bfloat16), 'mode').astype(jnp.float32)  66.5 us
    psum x1, waiting for transfers between devices, on_device(): summed = lax.psum(core.astype(jnp.bfloat16), 'mode').astype(jnp.float32)  64.6 us
    dynamic_update_slice x2, local copies, waits for them, and re-layouts, deposit(): lax.dynamic_update_slice(extended, current + block, (anchor, row_at, col_...  25 us
    dot_general x16, matrix products, left_mult(): jnp.einsum('uv,kvw->kuw', matrix, signal, preferred_element_type=jnp.floa...  23.1 us
    dot_general x16, matrix products, right_mult(): jnp.einsum('kuv,vw->kuw', signal, matrix, preferred_element_type=jnp.floa...  20.7 us
    ppermute x4, starting transfers between devices, padded_2(): lax.ppermute(lax.slice_in_dim(block, 0, width, axis=dim), axis, backward)  12.2 us
    another operation x1, loops' own time, on_device(): extended = lax.fori_loop(0, live_count, apply_slot, extended)  10.2 us
    another operation x1, loops' own time, on_device(): lax.fori_loop(0, live_count, look, (far_store, exit_store, power_part))  10 us
  transfers between devices with their start and end apart: 10, of which 8 were waited for; matrix products, arithmetic and copies ran while one was open for 1% of the time, Pallas kernels for 0%

commit v1 on v0

--- a/solution.py
+++ b/solution.py
@@ -198,7 +198,7 @@
     core = inner[:, :, half_width : half_width + tile_cols]
     core = core.at[:, :, :half_width].add(cols_back[:, :, :half_width])
     core = core.at[:, :, tile_cols - half_width :].add(cols_back[:, :, 3 * half_width :])
-    summed = lax.psum(core.astype(jnp.bfloat16), "mode").astype(jnp.float32)
+    summed = jnp.sum(lax.all_gather(core.astype(jnp.bfloat16), "mode"), axis=0).astype(jnp.float32)
     return object_field + summed[:2] / (summed[2] + regularizer)
 
 

time: 310 us -> 274 us (0.88)
  the two profiles are of different devices: /device:TPU:2 before, /device:TPU:198 now
where the time goes in v1:
time: 274 us; the launch traced here: 273 us
  waiting for transfers between devices  139 us (51%)
  starting transfers between devices  27.7 us (10%)
  local copies, waits for them, and re-layouts  27.2 us (10%)
  matrix products  21.9 us (8%)
  blocking collectives  21 us (8%)
  between operations  13.7 us (5%)
  other arithmetic  11.6 us (4%)
  loops' own time  10.8 us (4%)
    psum x1, waiting for transfers between devices, on_device(): lax.psum(power_part.astype(jnp.bfloat16), 'mode').astype(jnp.float32)  71.6 us
    ppermute x4, waiting for transfers between devices, padded_2(): lax.ppermute(lax.slice_in_dim(block, 0, width, axis=dim), axis, backward)  58.2 us
    all_gather x1, blocking collectives, on_device(): lax.all_gather(core.astype(jnp.bfloat16), 'mode')  21 us
    ppermute x4, starting transfers between devices, padded_2(): lax.ppermute(lax.slice_in_dim(block, block.shape[dim] - width, None, axis...  18.3 us
    dot_general x8, matrix products, left_mult(): jnp.einsum('uv,kvw->kuw', matrix, signal, preferred_element_type=jnp.floa...  11.6 us
    dynamic_update_slice x1, local copies, waits for them, and re-layouts, deposit(): lax.dynamic_update_slice(extended, current + block, (anchor, row_at, col_...  11.5 us
    dot_general x8, matrix products, right_mult(): jnp.einsum('kuv,vw->kuw', signal, matrix, preferred_element_type=jnp.floa...  10.3 us
    ppermute x4, waiting for transfers between devices, padded_2(): lax.ppermute(lax.slice_in_dim(block, block.shape[dim] - width, None, axis...  9.48 us
  transfers between devices with their start and end apart: 9, of which 9 were waited for; matrix products, arithmetic and copies ran while one was open for 1% of the time, Pallas kernels for 0%

profile of v1, /device:TPU:198, one launch (start us, length us, event | category | flops | bytes accessed | tf_op | source)
XLA Modules:
  0.0 273.1 jit_solution(16836496967743407958)
XLA Ops:
  7.7 1.9 collective-permute-start.1
  9.6 2.4 collective-permute-start
  12.1 3.8 %collective-permute-done = bf16[2,128,256]{1,2,0:T(8,128)(2,1)S(1)} collective-permute-done((bf16[2,128,256]{1,2,0:T(8,128)(2,1)S(1)}, bf16[2,128,256]{1,2,0:T(8,128)(2,1)S(1)}, u32[]{:S(2)}, u32[]{:S(2)}) %collective-permute-start) | collective-permute-done | bytes 131104 | tf_op jit(solution)/shard_map/ppermute | solution.py:16
  16.0 7.6 %collective-permute-start.2 = (bf16[2,384,128]{1,2,0:T(8,128)(2,1)S(1)}, bf16[2,384,128]{1,2,0:T(8,128)(2,1)S(1)}, u32[]{:S(2)}, u32[]{:S(2)}) collective-permute-start(bf16[2,384,128]{1,2,0:T(8,128)(2,1)S(1)} %get-tuple-element.547), channel_id=1, source_target_pairs={{0,4},{4,8},{8,12},{12,16},{16,20},{20,24},{24,28},{1,5},{5,9},{9,... | collective-permute-start | bytes 589832 | tf_op jit(solution)/shard_map/ppermute | solution.py:16
  23.7 1.9 collective-permute-start.3
  26.7 2.0 collective-permute-done.2
  29.3 10.2 %collective-permute-done.3 = bf16[2,384,128]{1,2,0:T(8,128)(2,1)} collective-permute-done((bf16[2,384,128]{1,2,0:T(8,128)(2,1)S(1)}, bf16[2,384,128]{1,2,0:T(8,128)(2,1)}, u32[]{:S(2)}, u32[]{:S(2)}) %collective-permute-start.3) | collective-permute-done | bytes 196640 | tf_op jit(solution)/shard_map/ppermute | solution.py:19
  44.0 19.9 %while.36 = (s32[]{:T(128)}, f32[2,2,2,256,256]{4,3,2,1,0:T(8,128)}, bf16[2,2,2,256,256]{3,4,2,1,0:T(8,128)(2,1)}, bf16[2,256,256]{1,2,0:T(8,128)(2,1)}, s32[]{:...) while((s32[]{:T(128)}, ...), condition=%wide.region_2.3_spmd.clone.clone, body=%wide.region_0.2_spmd.clone.clone.sunk | while | flops 550305792 | bytes 17170740 | solution.py:157
  57.8 1.9 add_reduce_fusion.5
  64.0 2.0 add_reduce_fusion.2
  66.0 71.6 %all-reduce.2.cloned.1.call-done = bf16[2,256,256]{1,2,0:T(8,128)(2,1)} async-done(((bf16[2,256,256]{1,2,0:T(8,128)(2,1)}), bf16[2,256,256]{1,2,0:T(8,128)(2,1)}) %all-reduce.2.cloned.1.call-update) | async-done | bytes 262160 | tf_op jit(solution)/shard_map/psum | solution.py:160
  137.6 1.8 convert_element_type.194
  139.6 38.7 %while.37 = (s32[]{:T(128)}, f32[3,384,512]{2,1,0:T(8,128)S(1)}, s32[]{:T(128)}, s32[1,1,2,2]{3,2,1,0:T(2,128)S(1)}, f32[2,2,2,256,256]{4,3,2,1,0:T(8,128)}, /*i...) while((s32[]{:T(128)}, f32[3,384,512]{2,1,0:T(8,128)S(1)}, ...), condition=%wide.region_8.9_spmd.clone.clone, body=%wide.region_5.8_spmd.clone.clone.sunk | while | flops 550371328 | bytes 32899572 | solution.py:182
  153.0 2.2 fusion.268
  155.2 2.3 fusion.269
  166.1 11.5 %dynamic_update_slice.35 = f32[3,384,512]{2,1,0:T(8,128)S(1)} dynamic-update-slice(f32[3,384,512]{2,1,0:T(8,128)S(1)} %get-tuple-element.772, f32[3,256,256]{2,1,0:T(8,128)S(1)} %maximum_add_fusion.2, s32[]{:T(128)} %constant.212.clone.1..sunk.1, s32[]{:T(128)S(6)} %select_n.188, s32[]{:T(128)S(6)} %select_n.189) | dynamic-update-slice | bytes 1572868 | tf_op jit(solution)/shard_map/while/body/dynamic_update_slice | solution.py:131
  178.5 1.9 collective-permute-start.4
  180.4 3.6 %collective-permute-start.5 = (bf16[3,128,512]{2,1,0:T(8,128)(2,1)S(1)}, bf16[3,128,512]{2,1,0:T(8,128)(2,1)S(1)}, u32[]{:S(2)}, u32[]{:S(2)}) collective-permute-start(bf16[3,128,512]{2,1,0:T(8,128)(2,1)S(1)} %get-tuple-element.542), channel_id=1, source_target_pairs={{32,0},{64,32},{96,64},{128,96},{160,128},{192,160},{224,192},{256... | collective-permute-start | bytes 1179656 | tf_op jit(solution)/shard_map/ppermute | solution.py:19
  184.1 3.5 %collective-permute-done.4 = bf16[3,128,512]{2,1,0:T(8,128)(2,1)S(1)} collective-permute-done((bf16[3,128,512]{2,1,0:T(8,128)(2,1)S(1)}, bf16[3,128,512]{2,1,0:T(8,128)(2,1)S(1)}, u32[]{:S(2)}, u32[]{:S(2)}) %collective-permute-start.4) | collective-permute-done | bytes 393248 | tf_op jit(solution)/shard_map/ppermute | solution.py:16
  187.6 37.6 %collective-permute-done.5 = bf16[3,128,512]{2,1,0:T(8,128)(2,1)S(1)} collective-permute-done((bf16[3,128,512]{2,1,0:T(8,128)(2,1)S(1)}, bf16[3,128,512]{2,1,0:T(8,128)(2,1)S(1)}, u32[]{:S(2)}, u32[]{:S(2)}) %collective-permute-start.5) | collective-permute-done | bytes 393248 | tf_op jit(solution)/shard_map/ppermute | solution.py:19
  225.4 6.3 %collective-permute-start.6 = (bf16[3,128,128]{2,1,0:T(8,128)(2,1)S(1)}, bf16[3,128,128]{2,1,0:T(8,128)(2,1)S(1)}, u32[]{:S(2)}, u32[]{:S(2)}) collective-permute-start(bf16[3,128,128]{2,1,0:T(8,128)(2,1)S(1)} %get-tuple-element.545), channel_id=1, source_target_pairs={{0,4},{4,8},{8,12},{12,16},{16,20},{20,24},{24,28},{1,5},{5,9},{9,... | collective-permute-start | bytes 294920 | tf_op jit(solution)/shard_map/ppermute | solution.py:16
  231.7 1.9 collective-permute-start.7
  233.9 10.4 %collective-permute-done.7 = bf16[3,128,128]{2,1,0:T(8,128)(2,1)S(1)} collective-permute-done((bf16[3,128,128]{2,1,0:T(8,128)(2,1)S(1)}, bf16[3,128,128]{2,1,0:T(8,128)(2,1)S(1)}, u32[]{:S(2)}, u32[]{:S(2)}) %collective-permute-start.7) | collective-permute-done | bytes 98336 | tf_op jit(solution)/shard_map/ppermute | solution.py:19
  244.4 21.0 %all-gather = bf16[12,128,256]{2,1,0:T(8,128)(2,1)S(1)} all-gather(bf16[3,128,256]{2,1,0:T(8,128)(2,1)S(1)} %convert_element_type.197), channel_id=2, replica_groups=mesh['tx'=16,'ty'=8,'mode'=4] {'mode'}, dimensions={0}, use_global_device_ids=true | all-gather | bytes 983040 | tf_op jit(solution)/shard_map/all_gather | solution.py:201
  (91 shorter events, 39.4 us)
Async XLA Ops:
  6.5 19.1 %copy-start.8 = (f32[2,2,256,256]{3,2,1,0:T(8,128)S(1)}, f32[2,2,256,256]{3,2,1,0:T(8,128)}, u32[]{:S(2)}) copy-start(f32[2,2,256,256]{3,2,1,0:T(8,128)} %param.22) | copy-start | bytes 3145732
  6.5 131.0 %all-reduce.2.cloned.1.call-start = ((), (), s32[]{:S(2)}) async-start(), calls=%async_computation | async-start | bytes 524288 | tf_op jit(solution)/shard_map/psum | solution.py:160
  7.7 4.4 %collective-permute-start.1 = (bf16[2,128,256]{1,2,0:T(8,128)(2,1)S(1)}, bf16[2,128,256]{1,2,0:T(8,128)(2,1)S(1)}, u32[]{:S(2)}, u32[]{:S(2)}) collective-permute-start(bf16[2,128,256]{1,2,0:T(8,128)(2,1)S(1)} %copy.29), channel_id=1, source_target_pairs={{32,0},{64,32},{96,64},{128,96},{160,128},{192,160},{224,192},{256... | collective-permute-start | bytes 393224 | tf_op jit(solution)/shard_map/ppermute | solution.py:19
  9.6 6.3 %collective-permute-start = (bf16[2,128,256]{1,2,0:T(8,128)(2,1)S(1)}, bf16[2,128,256]{1,2,0:T(8,128)(2,1)S(1)}, u32[]{:S(2)}, u32[]{:S(2)}) collective-permute-start(bf16[2,128,256]{1,2,0:T(8,128)(2,1)S(1)} %copy.29), channel_id=1, source_target_pairs={{0,32},{32,64},{64,96},{96,128},{128,160},{160,192},{192,224},{224... | collective-permute-start | bytes 393224 | tf_op jit(solution)/shard_map/ppermute | solution.py:16
  12.1 13.6 %copy-start.10 = (bf16[2,128,256]{1,2,0:T(8,128)(2,1)}, bf16[2,128,256]{1,2,0:T(8,128)(2,1)S(1)}, u32[]{:S(2)}) copy-start(bf16[2,128,256]{1,2,0:T(8,128)(2,1)S(1)} %collective-permute-done.1) | copy-start | bytes 393220
  15.9 9.8 %copy-start.12 = (bf16[2,128,256]{1,2,0:T(8,128)(2,1)}, bf16[2,128,256]{1,2,0:T(8,128)(2,1)S(1)}, u32[]{:S(2)}) copy-start(bf16[2,128,256]{1,2,0:T(8,128)(2,1)S(1)} %collective-permute-done) | copy-start | bytes 393220
  16.0 12.6 %collective-permute-start.2 = (bf16[2,384,128]{1,2,0:T(8,128)(2,1)S(1)}, bf16[2,384,128]{1,2,0:T(8,128)(2,1)S(1)}, u32[]{:S(2)}, u32[]{:S(2)}) collective-permute-start(bf16[2,384,128]{1,2,0:T(8,128)(2,1)S(1)} %get-tuple-element.547), channel_id=1, source_target_pairs={{0,4},{4,8},{8,12},{12,16},{16,20},{20,24},{24,28},{1,5},{5,9},{9,... | collective-permute-start | bytes 589832 | tf_op jit(solution)/shard_map/ppermute | solution.py:16
  23.7 15.9 %collective-permute-start.3 = (bf16[2,384,128]{1,2,0:T(8,128)(2,1)S(1)}, bf16[2,384,128]{1,2,0:T(8,128)(2,1)}, u32[]{:S(2)}, u32[]{:S(2)}) collective-permute-start(bf16[2,384,128]{1,2,0:T(8,128)(2,1)S(1)} %get-tuple-element.548), channel_id=1, source_target_pairs={{4,0},{8,4},{12,8},{16,12},{20,16},{24,20},{28,24},{5,1},{9,5},{13... | collective-permute-start | bytes 589832 | tf_op jit(solution)/shard_map/ppermute | solution.py:19
  25.7 0.8 copy-start.1
  25.7 16.7 %copy-start.3 = (f32[2,256,256]{2,1,0:T(8,128)}, f32[2,256,256]{2,1,0:T(8,128)S(1)}, u32[]{:S(2)}) copy-start(f32[2,256,256]{2,1,0:T(8,128)S(1)} %get-tuple-element.762) | copy-start | bytes 1572868
  25.8 13.8 %copy-start.11 = (bf16[2,128,256]{1,2,0:T(8,128)(2,1)S(1)}, bf16[2,128,256]{1,2,0:T(8,128)(2,1)}, u32[]{:S(2)}) copy-start(bf16[2,128,256]{1,2,0:T(8,128)(2,1)} %copy-done.10) | copy-start | bytes 393220
  25.8 13.8 %copy-start.13 = (bf16[2,128,256]{1,2,0:T(8,128)(2,1)S(1)}, bf16[2,128,256]{1,2,0:T(8,128)(2,1)}, u32[]{:S(2)}) copy-start(bf16[2,128,256]{1,2,0:T(8,128)(2,1)} %copy-done.12) | copy-start | bytes 393220
  40.7 3.3 %copy-start.15 = (s32[1,1,2,2]{3,2,1,0:T(2,128)S(1)}, s32[1,1,2,2]{3,2,1,0:T(2,128)}, u32[]{:S(2)}) copy-start(s32[1,1,2,2]{3,2,1,0:T(2,128)} %param.24) | copy-start | bytes 52
  153.0 4.5 %copy-start.5 = (f32[1,1,2,256,256]{3,4,2,1,0:T(8,128)S(1)}, f32[1,1,2,256,256]{3,4,2,1,0:T(8,128)}, u32[]{:S(2)}) copy-start(f32[1,1,2,256,256]{3,4,2,1,0:T(8,128)} %copy.61) | copy-start | bytes 1572868 | tf_op jit(solution)/shard_map/while
  153.0 4.5 %copy-start.7 = (f32[256,256]{0,1:T(8,128)S(1)}, f32[256,256]{0,1:T(8,128)}, u32[]{:S(2)}) copy-start(f32[256,256]{0,1:T(8,128)} %fusion.264) | copy-start | bytes 786436 | tf_op jit(solution)/shard_map/while
  158.7 3.6 %copy-start.6 = (bf16[1,1,2,256,256]{4,3,2,1,0:T(8,128)(2,1)S(1)}, bf16[1,1,2,256,256]{4,3,2,1,0:T(8,128)(2,1)}, u32[]{:S(2)}) copy-start(bf16[1,1,2,256,256]{4,3,2,1,0:T(8,128)(2,1)} %copy.64) | copy-start | bytes 786436 | tf_op jit(solution)/shard_map/while
  161.1 2.4 copy-start
  161.1 2.4 copy-start.2
  161.1 2.4 copy-start.4
  178.5 9.1 %collective-permute-start.4 = (bf16[3,128,512]{2,1,0:T(8,128)(2,1)S(1)}, bf16[3,128,512]{2,1,0:T(8,128)(2,1)S(1)}, u32[]{:S(2)}, u32[]{:S(2)}) collective-permute-start(bf16[3,128,512]{2,1,0:T(8,128)(2,1)S(1)} %get-tuple-element.541), channel_id=1, source_target_pairs={{0,32},{32,64},{64,96},{96,128},{128,160},{160,192},{192,224},{224... | collective-permute-start | bytes 1179656 | tf_op jit(solution)/shard_map/ppermute | solution.py:16
  180.4 44.7 %collective-permute-start.5 = (bf16[3,128,512]{2,1,0:T(8,128)(2,1)S(1)}, bf16[3,128,512]{2,1,0:T(8,128)(2,1)S(1)}, u32[]{:S(2)}, u32[]{:S(2)}) collective-permute-start(bf16[3,128,512]{2,1,0:T(8,128)(2,1)S(1)} %get-tuple-element.542), channel_id=1, source_target_pairs={{32,0},{64,32},{96,64},{128,96},{160,128},{192,160},{224,192},{256... | collective-permute-start | bytes 1179656 | tf_op jit(solution)/shard_map/ppermute | solution.py:19
  225.4 8.5 %collective-permute-start.6 = (bf16[3,128,128]{2,1,0:T(8,128)(2,1)S(1)}, bf16[3,128,128]{2,1,0:T(8,128)(2,1)S(1)}, u32[]{:S(2)}, u32[]{:S(2)}) collective-permute-start(bf16[3,128,128]{2,1,0:T(8,128)(2,1)S(1)} %get-tuple-element.545), channel_id=1, source_target_pairs={{0,4},{4,8},{8,12},{12,16},{16,20},{20,24},{24,28},{1,5},{5,9},{9,... | collective-permute-start | bytes 294920 | tf_op jit(solution)/shard_map/ppermute | solution.py:16
  231.7 12.5 %collective-permute-start.7 = (bf16[3,128,128]{2,1,0:T(8,128)(2,1)S(1)}, bf16[3,128,128]{2,1,0:T(8,128)(2,1)S(1)}, u32[]{:S(2)}, u32[]{:S(2)}) collective-permute-start(bf16[3,128,128]{2,1,0:T(8,128)(2,1)S(1)} %get-tuple-element.546), channel_id=1, source_target_pairs={{4,0},{8,4},{12,8},{16,12},{20,16},{24,20},{28,24},{5,1},{9,5},{13... | collective-permute-start | bytes 294920 | tf_op jit(solution)/shard_map/ppermute | solution.py:19
  244.3 21.3 %copy-start.9 = (f32[2,128,256]{2,1,0:T(8,128)S(1)}, f32[2,128,256]{2,1,0:T(8,128)}, u32[]{:S(2)}) copy-start(f32[2,128,256]{2,1,0:T(8,128)} %param.21) | copy-start | bytes 786436
  (1 other events, 0.7 us)
Sparse Core Ops, SparseCore 0:
  64.1 73.4 all-reduce.1
